TPU v7x, 256 devices: a whole 4x4x8 slice. The times are simulated.
256 devices in a mesh: grp: 2 (over x_hi), row: 16 (over z, core), col: 8 (over y, x_lo).
Axes of the slice: x: 4 (x_hi: 2, x_lo: 2; x = x_hi * 2 + x_lo), y: 4, z: 8, core: 2. Of those that a mesh axis runs over, the one named last changes fastest.
Arguments:
- vectors: float32 [64, 256, 2048], P('grp', 'row', 'col'), may hold values from -6 to 6
- disorder: float32 [256, 2048], P('row', 'col'), may hold values from -1.5 to 1.5
Outputs:
- cheb_prev: float32 [64, 256, 2048], P('grp', 'row', 'col')
- cheb_last: float32 [64, 256, 2048], P('grp', 'row', 'col')
- moments: float32 [17], replicated
All inputs are finite; a program needn't handle non-finite values.
Results may differ from a plain program's by a relative error of at most 0.0001.
Values sent between devices are 32-bit elements; how exact they have to be, the bound alone decides.
A program may use at most 64 MiB of HBM per device.

v0:
```python
import functools

import jax
import jax.numpy as jnp
from jax import lax
from jax.sharding import Mesh
from jax.sharding import PartitionSpec as P

STEPS = 8
ROW = ("row_0", "row_1")
COL = ("col_0", "col_1")
GRP_ROW_COL = ("grp", "row_0", "row_1", "col_0", "col_1")


SCALE = 4.6


def extended(block, sides, width):
    for axis, dim in sides:
        count = lax.axis_size(axis)
        forward = [(i, i + 1) for i in range(count - 1)]
        forward.append((count - 1, 0))
        backward = [(target, source) for source, target in forward]
        low = lax.ppermute(
            lax.slice_in_dim(block, block.shape[dim] - width, None, axis=dim), axis, forward
        )
        high = lax.ppermute(lax.slice_in_dim(block, 0, width, axis=dim), axis, backward)
        block = jnp.concatenate([low, block, high], axis=dim)
    return block


def by_axis(x, axes):
    return functools.reduce(lax.psum, axes, x)


def inner_hop(field, dis_part, even_part):
    left = field[:, 1:-1, :-2]
    right = field[:, 1:-1, 2:]
    below = field[:, 2:, 1:-1]
    above = field[:, :-2, 1:-1]
    center = field[:, 1:-1, 1:-1]
    vertical = jnp.where(even_part, below, above)
    return (dis_part * center - (left + right + vertical)) / SCALE


def body(vectors, disorder):
    vecs, rows_here, cols_here = vectors.shape
    count = float(
        vecs
        * lax.axis_size("grp")
        * rows_here
        * lax.axis_size(ROW)
        * cols_here
        * lax.axis_size(COL)
    )
    margin = 4
    dis_pad = extended(disorder, ((ROW, 0), (COL, 1)), margin)
    rows = lax.broadcasted_iota(jnp.int32, dis_pad.shape, 0)
    cols = lax.broadcasted_iota(jnp.int32, dis_pad.shape, 1)
    even_pad = (rows + cols) % 2 == 0

    def advance(field):
        extra = (field.shape[1] - rows_here) // 2
        start = margin - extra
        stop_r = start + field.shape[1] - 1
        stop_c = start + field.shape[2] - 1
        dis_part = dis_pad[start + 1 : stop_r, start + 1 : stop_c]
        even_part = even_pad[start + 1 : stop_r, start + 1 : stop_c][None]
        return inner_hop(field, dis_part, even_part)

    def interior(field):
        extra = (field.shape[1] - rows_here) // 2
        return field[:, extra : extra + rows_here, extra : extra + cols_here]

    older = vectors
    newer = vectors
    squares = [jnp.sum(vectors * vectors)]
    crosses = []
    for rounds in range(STEPS // margin):
        padded_old, padded_new = (
            extended(older, ((ROW, 1), (COL, 2)), margin),
            extended(newer, ((ROW, 1), (COL, 2)), margin),
        )
        for inner in range(margin):
            if rounds == 0 and inner == 0:
                latest = advance(padded_new)
            else:
                latest = 2.0 * advance(padded_new) - padded_old[:, 1:-1, 1:-1]
            padded_old = padded_new[:, 1:-1, 1:-1]
            padded_new = latest
            kept_new = interior(padded_new)
            kept_old = interior(padded_old)
            squares.append(jnp.sum(kept_new * kept_new))
            crosses.append(jnp.sum(kept_new * kept_old))
        older, newer = (padded_old, padded_new)
    joined = by_axis(jnp.concatenate([jnp.stack(squares), jnp.stack(crosses)]), GRP_ROW_COL)
    total_squares = joined[: STEPS + 1]
    total_crosses = joined[STEPS + 1 :]
    total_squares = total_squares / count
    total_crosses = total_crosses / count
    first = total_squares[0]
    second = total_crosses[0]
    values = [first, second]
    for index in range(1, STEPS + 1):
        values.append(2.0 * total_squares[index] - first)
        if index < STEPS:
            values.append(2.0 * total_crosses[index] - second)
    return (older, newer, jnp.stack(values))


def solution(mesh):
    torus = Mesh(
        mesh.devices.reshape(mesh.shape["grp"], 8, 2, 4, 2),
        ("grp", "row_0", "row_1", "col_0", "col_1"),
    )
    in_specs = (P("grp", ROW, COL), P(ROW, COL))
    out_specs = (P("grp", ROW, COL), P("grp", ROW, COL), P())
    return jax.shard_map(body, mesh=torus, in_specs=in_specs, out_specs=out_specs, check_vma=False)
```

profile of v0, /device:TPU:1, one launch (start us, length us, event | category | flops | bytes accessed | tf_op | source)
XLA Modules:
  0.0 163.2 jit_solution(12153578722486552633)
XLA Ops:
  1.4 3.0 %collective-permute-start = (f32[4,256]{1,0:T(4,128)S(1)}, f32[4,256]{1,0:T(4,128)S(1)}, u32[]{:S(2)}, u32[]{:S(2)}) collective-permute-start(f32[4,256]{1,0:T(4,128)S(1)} %get-tuple-element.46), channel_id=1, source_target_pairs={{0,8},{8,16},{16,24},{24,32},{32,40},{40,48},{48,56},{56,64},{64,7... | collective-permute-start | bytes 12296 | tf_op jit(solution)/shard_map/ppermute | solution.py:24
  7.2 2.1 %collective-permute-start.5 = (f32[32,4,256]{2,1,0:T(4,128)S(1)}, f32[32,4,256]{2,1,0:T(4,128)S(1)}, u32[]{:S(2)}, u32[]{:S(2)}) collective-permute-start(f32[32,4,256]{2,1,0:T(4,128)S(1)} %get-tuple-element.43), channel_id=1, source_target_pairs={{8,0},{16,8},{24,16},{32,24},{40,32},{48,40},{56,48},{64,56},{72,6... | collective-permute-start | bytes 393224 | tf_op jit(solution)/shard_map/ppermute | solution.py:27
  11.7 2.5 %collective-permute-start.3 = (f32[24,4]{1,0:T(8,128)S(1)}, f32[24,4]{1,0:T(8,128)S(1)}, u32[]{:S(2)}, u32[]{:S(2)}) collective-permute-start(f32[24,4]{1,0:T(8,128)S(1)} %get-tuple-element.45), channel_id=1, source_target_pairs={{1,0},{2,1},{3,2},{4,3},{5,4},{6,5},{7,6},{0,7},{9,8},{10,9},{11,1... | collective-permute-start | bytes 1160 | tf_op jit(solution)/shard_map/ppermute | solution.py:27
  15.6 3.6 %collective-permute-start.7 = (f32[32,24,4]{2,1,0:T(8,128)S(1)}, f32[32,24,4]{2,1,0:T(8,128)S(1)}, u32[]{:S(2)}, u32[]{:S(2)}) collective-permute-start(f32[32,24,4]{2,1,0:T(8,128)S(1)} %get-tuple-element.39), channel_id=1, source_target_pairs={{1,0},{2,1},{3,2},{4,3},{5,4},{6,5},{7,6},{0,7},{9,8},{10,9},{11,1... | collective-permute-start | bytes 36872 | tf_op jit(solution)/shard_map/ppermute | solution.py:27
  19.6 5.8 %collective-permute-done.6 = f32[32,24,4]{2,1,0:T(8,128)S(1)} collective-permute-done((f32[32,24,4]{2,1,0:T(8,128)S(1)}, f32[32,24,4]{2,1,0:T(8,128)S(1)}, u32[]{:S(2)}, u32[]{:S(2)}) %collective-permute-start.6) | collective-permute-done | bytes 12320 | tf_op jit(solution)/shard_map/ppermute | solution.py:24
  25.4 5.8 %collective-permute-done.7 = f32[32,24,4]{2,1,0:T(8,128)S(1)} collective-permute-done((f32[32,24,4]{2,1,0:T(8,128)S(1)}, f32[32,24,4]{2,1,0:T(8,128)S(1)}, u32[]{:S(2)}, u32[]{:S(2)}) %collective-permute-start.7) | collective-permute-done | bytes 12320 | tf_op jit(solution)/shard_map/ppermute | solution.py:27
  37.2 4.4 %collective-permute-start.8 = (f32[32,4,256]{2,1,0:T(4,128)S(1)}, f32[32,4,256]{2,1,0:T(4,128)S(1)}, u32[]{:S(2)}, u32[]{:S(2)}) collective-permute-start(f32[32,4,256]{2,1,0:T(4,128)S(1)} %get-tuple-element.40), channel_id=1, source_target_pairs={{0,8},{8,16},{16,24},{24,32},{32,40},{40,48},{48,56},{56,64},{64,7... | collective-permute-start | bytes 393224 | tf_op jit(solution)/shard_map/ppermute | solution.py:24
  41.8 1.7 %collective-permute-start.12 = (f32[32,4,256]{2,1,0:T(4,128)S(1)}, f32[32,4,256]{2,1,0:T(4,128)S(1)}, u32[]{:S(2)}, u32[]{:S(2)}) collective-permute-start(f32[32,4,256]{2,1,0:T(4,128)S(1)} %get-tuple-element.30), channel_id=1, source_target_pairs={{0,8},{8,16},{16,24},{24,32},{32,40},{40,48},{48,56},{56,64},{64,7... | collective-permute-start | bytes 393224 | tf_op jit(solution)/shard_map/ppermute | solution.py:24
  43.6 2.4 %collective-permute-start.13 = (f32[32,4,256]{2,1,0:T(4,128)S(1)}, f32[32,4,256]{2,1,0:T(4,128)S(1)}, u32[]{:S(2)}, u32[]{:S(2)}) collective-permute-start(f32[32,4,256]{2,1,0:T(4,128)S(1)} %get-tuple-element.31), channel_id=1, source_target_pairs={{8,0},{16,8},{24,16},{32,24},{40,32},{48,40},{56,48},{64,56},{72,6... | collective-permute-start | bytes 393224 | tf_op jit(solution)/shard_map/ppermute | solution.py:27
  46.7 3.2 %collective-permute-start.11 = (f32[32,24,4]{2,1,0:T(8,128)S(1)}, f32[32,24,4]{2,1,0:T(8,128)S(1)}, u32[]{:S(2)}, u32[]{:S(2)}) collective-permute-start(f32[32,24,4]{2,1,0:T(8,128)S(1)} %get-tuple-element.37), channel_id=1, source_target_pairs={{1,0},{2,1},{3,2},{4,3},{5,4},{6,5},{7,6},{0,7},{9,8},{10,9},{11,1... | collective-permute-start | bytes 36872 | tf_op jit(solution)/shard_map/ppermute | solution.py:27
  50.3 3.6 %collective-permute-start.15 = (f32[32,24,4]{2,1,0:T(8,128)S(1)}, f32[32,24,4]{2,1,0:T(8,128)S(1)}, u32[]{:S(2)}, u32[]{:S(2)}) collective-permute-start(f32[32,24,4]{2,1,0:T(8,128)S(1)} %get-tuple-element.35), channel_id=1, source_target_pairs={{1,0},{2,1},{3,2},{4,3},{5,4},{6,5},{7,6},{0,7},{9,8},{10,9},{11,1... | collective-permute-start | bytes 36872 | tf_op jit(solution)/shard_map/ppermute | solution.py:27
  53.9 2.4 %collective-permute-done.10 = f32[32,24,4]{2,1,0:T(8,128)S(1)} collective-permute-done((f32[32,24,4]{2,1,0:T(8,128)S(1)}, f32[32,24,4]{2,1,0:T(8,128)S(1)}, u32[]{:S(2)}, u32[]{:S(2)}) %collective-permute-start.10) | collective-permute-done | bytes 12320 | tf_op jit(solution)/shard_map/ppermute | solution.py:24
  56.3 7.3 %collective-permute-done.11 = f32[32,24,4]{2,1,0:T(8,128)S(1)} collective-permute-done((f32[32,24,4]{2,1,0:T(8,128)S(1)}, f32[32,24,4]{2,1,0:T(8,128)S(1)}, u32[]{:S(2)}, u32[]{:S(2)}) %collective-permute-start.11) | collective-permute-done | bytes 12320 | tf_op jit(solution)/shard_map/ppermute | solution.py:27
  64.3 8.8 %collective-permute-done.14 = f32[32,24,4]{2,1,0:T(8,128)S(1)} collective-permute-done((f32[32,24,4]{2,1,0:T(8,128)S(1)}, f32[32,24,4]{2,1,0:T(8,128)S(1)}, u32[]{:S(2)}, u32[]{:S(2)}) %collective-permute-start.14) | collective-permute-done | bytes 12320 | tf_op jit(solution)/shard_map/ppermute | solution.py:24
  73.1 7.3 %collective-permute-done.15 = f32[32,24,4]{2,1,0:T(8,128)S(1)} collective-permute-done((f32[32,24,4]{2,1,0:T(8,128)S(1)}, f32[32,24,4]{2,1,0:T(8,128)S(1)}, u32[]{:S(2)}, u32[]{:S(2)}) %collective-permute-start.15) | collective-permute-done | bytes 12320 | tf_op jit(solution)/shard_map/ppermute | solution.py:27
  80.4 2.1 %fusion.6 = f32[32,22,262]{2,1,0:T(8,128)S(1)} fusion(f32[32,24,4]{2,1,0:T(8,128)S(1)} %collective-permute-done.15, f32[32,24,4]{2,1,0:T(8,128)S(1)} %collective-permute-done.14, f32[32,4,256]{2,1,0:T(4,128)S(1)} %collective-permute-done.13, f32[32,16,256]{2,1,0:T(8,128)S(1)} %get-tuple-element.32, f32[32,4,256]{2,1,0:T(4,128)S(1)} %collective-permute-done.12, ...), kind=kLoop, calls=%fused_computation.15 | loop fusion | flops 2028928 | bytes 5266580 | tf_op jit(solution)/shard_map/sub | solution.py:88
  87.1 1.6 %multiply_reduce_fusion.1 = (f32[]{:T(128)}, f32[]{:T(128)}, f32[]{:T(128)}, f32[]{:T(128)}, f32[]{:T(128)}, /*index=5*/f32[]{:T(128)}, f32[]{:T(128)}, f32[]{:T...) fusion(f32[32,16,256]{2,1,0:T(8,128)S(1)} %get-tuple-element.29, ...), kind=kLoop, calls=%fused_computation.63 | loop fusion | flops 4194288 | bytes 4718656 | tf_op jit(solution)/shard_map/reduce_sum | solution.py:94
  88.8 10.7 %concatenate.35 = f32[17]{0:T(128)S(1)} concatenate(f32[1]{0:T(128)} %bitcast, f32[1]{0:T(128)} %bitcast.1, f32[1]{0:T(128)} %bitcast.2, f32[1]{0:T(128)} %bitcast.3, f32[1]{0:T(128)} %bitcast.4, f32[1]{0:T(128)} %bitcast.5, f32[1]{0:T(128)} %bitcast.6, f32[1]{0:T(128)} %bitcast.7, f32[1]{0:T(128)} %bitcast.8, f32[1]{0:T(128)} %bitcast.9, f32[1]{0:T(128)} %bitcast.10, ...), dimensions={0} | concatenate | bytes 136 | tf_op jit(solution)/shard_map/concatenate | solution.py:96
  99.4 5.3 %psum.35 = f32[17]{0:T(128)S(1)} all-reduce(f32[17]{0:T(128)S(1)} %concatenate.35), channel_id=1, replica_groups=mesh['grp'=2,'row_0'=8,'row_1'=2,'col_0'=4,'col_1'=2] {'grp'}, use_global_device_ids=true, to_apply=%region_17.18 | all-reduce | flops 17 | bytes 136 | tf_op jit(solution)/shard_map/psum | solution.py:33
  104.7 18.7 %psum.36 = f32[17]{0:T(128)S(1)} all-reduce(f32[17]{0:T(128)S(1)} %psum.35), channel_id=1, replica_groups=mesh['grp'=2,'row_0'=8,'row_1'=2,'col_0'=4,'col_1'=2] {'row_0'}, use_global_device_ids=true, to_apply=%region_18.19 | all-reduce | flops 17 | bytes 136 | tf_op jit(solution)/shard_map/psum | solution.py:33
  123.4 7.3 %psum.37 = f32[17]{0:T(128)S(1)} all-reduce(f32[17]{0:T(128)S(1)} %psum.36), channel_id=1, replica_groups=mesh['grp'=2,'row_0'=8,'row_1'=2,'col_0'=4,'col_1'=2] {'row_1'}, use_global_device_ids=true, to_apply=%region_19.20 | all-reduce | flops 17 | bytes 136 | tf_op jit(solution)/shard_map/psum | solution.py:33
  130.7 7.3 %psum.38 = f32[17]{0:T(128)S(1)} all-reduce(f32[17]{0:T(128)S(1)} %psum.37), channel_id=1, replica_groups=mesh['grp'=2,'row_0'=8,'row_1'=2,'col_0'=4,'col_1'=2] {'col_0'}, use_global_device_ids=true, to_apply=%region_20.21 | all-reduce | flops 17 | bytes 136 | tf_op jit(solution)/shard_map/psum | solution.py:33
  138.0 3.8 %psum.39 = f32[17]{0:T(128)S(1)} all-reduce(f32[17]{0:T(128)S(1)} %psum.38), channel_id=1, replica_groups=mesh['grp'=2,'row_0'=8,'row_1'=2,'col_0'=4,'col_1'=2] {'col_1'}, use_global_device_ids=true, to_apply=%region_21.22 | all-reduce | flops 17 | bytes 136 | tf_op jit(solution)/shard_map/psum | solution.py:33
  161.3 1.9 %stack.86 = f32[17]{0:T(128)} concatenate(f32[1]{0:T(128)} %get-tuple-element.56, f32[1]{0:T(128)} %get-tuple-element.65, f32[1]{0:T(128)S(6)} %sub.120, f32[1]{0:T(128)S(6)} %sub.121, f32[1]{0:T(128)S(6)} %sub.122, f32[1]{0:T(128)S(6)} %sub.123, f32[1]{0:T(128)S(6)} %sub.124, f32[1]{0:T(128)S(6)} %sub.125, f32[1]{0:T(128)S(6)} %sub.126, f32[1]{0:T(128)S(6)} %sub.127, ...), dimensions={0} | concatenate | bytes 136 | tf_op jit(solution)/shard_map/stack | solution.py:108
  (58 shorter events, 21.2 us)
Async XLA Ops:
  1.4 8.3 %collective-permute-start = (f32[4,256]{1,0:T(4,128)S(1)}, f32[4,256]{1,0:T(4,128)S(1)}, u32[]{:S(2)}, u32[]{:S(2)}) collective-permute-start(f32[4,256]{1,0:T(4,128)S(1)} %get-tuple-element.46), channel_id=1, source_target_pairs={{0,8},{8,16},{16,24},{24,32},{32,40},{40,48},{48,56},{56,64},{64,7... | collective-permute-start | bytes 12296 | tf_op jit(solution)/shard_map/ppermute | solution.py:24
  4.4 5.3 %collective-permute-start.1 = (f32[4,256]{1,0:T(4,128)S(1)}, f32[4,256]{1,0:T(4,128)S(1)}, u32[]{:S(2)}, u32[]{:S(2)}) collective-permute-start(f32[4,256]{1,0:T(4,128)S(1)} %get-tuple-element.47), channel_id=1, source_target_pairs={{8,0},{16,8},{24,16},{32,24},{40,32},{48,40},{56,48},{64,56},{72,6... | collective-permute-start | bytes 12296 | tf_op jit(solution)/shard_map/ppermute | solution.py:27
  5.6 8.6 %collective-permute-start.4 = (f32[32,4,256]{2,1,0:T(4,128)S(1)}, f32[32,4,256]{2,1,0:T(4,128)S(1)}, u32[]{:S(2)}, u32[]{:S(2)}) collective-permute-start(f32[32,4,256]{2,1,0:T(4,128)S(1)} %get-tuple-element.42), channel_id=1, source_target_pairs={{0,8},{8,16},{16,24},{24,32},{32,40},{40,48},{48,56},{56,64},{64,7... | collective-permute-start | bytes 393224 | tf_op jit(solution)/shard_map/ppermute | solution.py:24
  7.2 7.0 %collective-permute-start.5 = (f32[32,4,256]{2,1,0:T(4,128)S(1)}, f32[32,4,256]{2,1,0:T(4,128)S(1)}, u32[]{:S(2)}, u32[]{:S(2)}) collective-permute-start(f32[32,4,256]{2,1,0:T(4,128)S(1)} %get-tuple-element.43), channel_id=1, source_target_pairs={{8,0},{16,8},{24,16},{32,24},{40,32},{48,40},{56,48},{64,56},{72,6... | collective-permute-start | bytes 393224 | tf_op jit(solution)/shard_map/ppermute | solution.py:27
  10.4 8.8 %collective-permute-start.2 = (f32[24,4]{1,0:T(8,128)S(1)}, f32[24,4]{1,0:T(8,128)S(1)}, u32[]{:S(2)}, u32[]{:S(2)}) collective-permute-start(f32[24,4]{1,0:T(8,128)S(1)} %get-tuple-element.44), channel_id=1, source_target_pairs={{0,1},{1,2},{2,3},{3,4},{4,5},{5,6},{6,7},{7,0},{8,9},{9,10},{10,1... | collective-permute-start | bytes 1160 | tf_op jit(solution)/shard_map/ppermute | solution.py:24
  11.7 7.6 %collective-permute-start.3 = (f32[24,4]{1,0:T(8,128)S(1)}, f32[24,4]{1,0:T(8,128)S(1)}, u32[]{:S(2)}, u32[]{:S(2)}) collective-permute-start(f32[24,4]{1,0:T(8,128)S(1)} %get-tuple-element.45), channel_id=1, source_target_pairs={{1,0},{2,1},{3,2},{4,3},{5,4},{6,5},{7,6},{0,7},{9,8},{10,9},{11,1... | collective-permute-start | bytes 1160 | tf_op jit(solution)/shard_map/ppermute | solution.py:27
  15.4 3.9 %copy-start.3 = (f32[16,256]{1,0:T(8,128)S(1)}, f32[16,256]{1,0:T(8,128)}, u32[]{:S(2)}) copy-start(f32[16,256]{1,0:T(8,128)} %param.3) | copy-start | bytes 49156
  15.4 15.8 %copy-start = (f32[32,16,256]{2,1,0:T(8,128)S(1)}, f32[32,16,256]{2,1,0:T(8,128)}, u32[]{:S(2)}) copy-start(f32[32,16,256]{2,1,0:T(8,128)} %param.2) | copy-start | bytes 1572868
  15.6 9.8 %collective-permute-start.6 = (f32[32,24,4]{2,1,0:T(8,128)S(1)}, f32[32,24,4]{2,1,0:T(8,128)S(1)}, u32[]{:S(2)}, u32[]{:S(2)}) collective-permute-start(f32[32,24,4]{2,1,0:T(8,128)S(1)} %get-tuple-element.38), channel_id=1, source_target_pairs={{0,1},{1,2},{2,3},{3,4},{4,5},{5,6},{6,7},{7,0},{8,9},{9,10},{10,1... | collective-permute-start | bytes 36872 | tf_op jit(solution)/shard_map/ppermute | solution.py:24
  15.6 15.5 %collective-permute-start.7 = (f32[32,24,4]{2,1,0:T(8,128)S(1)}, f32[32,24,4]{2,1,0:T(8,128)S(1)}, u32[]{:S(2)}, u32[]{:S(2)}) collective-permute-start(f32[32,24,4]{2,1,0:T(8,128)S(1)} %get-tuple-element.39), channel_id=1, source_target_pairs={{1,0},{2,1},{3,2},{4,3},{5,4},{6,5},{7,6},{0,7},{9,8},{10,9},{11,1... | collective-permute-start | bytes 36872 | tf_op jit(solution)/shard_map/ppermute | solution.py:27
  37.2 8.8 %collective-permute-start.8 = (f32[32,4,256]{2,1,0:T(4,128)S(1)}, f32[32,4,256]{2,1,0:T(4,128)S(1)}, u32[]{:S(2)}, u32[]{:S(2)}) collective-permute-start(f32[32,4,256]{2,1,0:T(4,128)S(1)} %get-tuple-element.40), channel_id=1, source_target_pairs={{0,8},{8,16},{16,24},{24,32},{32,40},{40,48},{48,56},{56,64},{64,7... | collective-permute-start | bytes 393224 | tf_op jit(solution)/shard_map/ppermute | solution.py:24
  41.6 4.4 %collective-permute-start.9 = (f32[32,4,256]{2,1,0:T(4,128)S(1)}, f32[32,4,256]{2,1,0:T(4,128)S(1)}, u32[]{:S(2)}, u32[]{:S(2)}) collective-permute-start(f32[32,4,256]{2,1,0:T(4,128)S(1)} %get-tuple-element.41), channel_id=1, source_target_pairs={{8,0},{16,8},{24,16},{32,24},{40,32},{48,40},{56,48},{64,56},{72,6... | collective-permute-start | bytes 393224 | tf_op jit(solution)/shard_map/ppermute | solution.py:27
  41.8 8.1 %collective-permute-start.12 = (f32[32,4,256]{2,1,0:T(4,128)S(1)}, f32[32,4,256]{2,1,0:T(4,128)S(1)}, u32[]{:S(2)}, u32[]{:S(2)}) collective-permute-start(f32[32,4,256]{2,1,0:T(4,128)S(1)} %get-tuple-element.30), channel_id=1, source_target_pairs={{0,8},{8,16},{16,24},{24,32},{32,40},{40,48},{48,56},{56,64},{64,7... | collective-permute-start | bytes 393224 | tf_op jit(solution)/shard_map/ppermute | solution.py:24
  43.6 6.4 %collective-permute-start.13 = (f32[32,4,256]{2,1,0:T(4,128)S(1)}, f32[32,4,256]{2,1,0:T(4,128)S(1)}, u32[]{:S(2)}, u32[]{:S(2)}) collective-permute-start(f32[32,4,256]{2,1,0:T(4,128)S(1)} %get-tuple-element.31), channel_id=1, source_target_pairs={{8,0},{16,8},{24,16},{32,24},{40,32},{48,40},{56,48},{64,56},{72,6... | collective-permute-start | bytes 393224 | tf_op jit(solution)/shard_map/ppermute | solution.py:27
  46.3 10.0 %collective-permute-start.10 = (f32[32,24,4]{2,1,0:T(8,128)S(1)}, f32[32,24,4]{2,1,0:T(8,128)S(1)}, u32[]{:S(2)}, u32[]{:S(2)}) collective-permute-start(f32[32,24,4]{2,1,0:T(8,128)S(1)} %get-tuple-element.36), channel_id=1, source_target_pairs={{0,1},{1,2},{2,3},{3,4},{4,5},{5,6},{6,7},{7,0},{8,9},{9,10},{10,1... | collective-permute-start | bytes 36872 | tf_op jit(solution)/shard_map/ppermute | solution.py:24
  46.7 16.8 %collective-permute-start.11 = (f32[32,24,4]{2,1,0:T(8,128)S(1)}, f32[32,24,4]{2,1,0:T(8,128)S(1)}, u32[]{:S(2)}, u32[]{:S(2)}) collective-permute-start(f32[32,24,4]{2,1,0:T(8,128)S(1)} %get-tuple-element.37), channel_id=1, source_target_pairs={{1,0},{2,1},{3,2},{4,3},{5,4},{6,5},{7,6},{0,7},{9,8},{10,9},{11,1... | collective-permute-start | bytes 36872 | tf_op jit(solution)/shard_map/ppermute | solution.py:27
  50.3 22.9 %collective-permute-start.14 = (f32[32,24,4]{2,1,0:T(8,128)S(1)}, f32[32,24,4]{2,1,0:T(8,128)S(1)}, u32[]{:S(2)}, u32[]{:S(2)}) collective-permute-start(f32[32,24,4]{2,1,0:T(8,128)S(1)} %get-tuple-element.34), channel_id=1, source_target_pairs={{0,1},{1,2},{2,3},{3,4},{4,5},{5,6},{6,7},{7,0},{8,9},{9,10},{10,1... | collective-permute-start | bytes 36872 | tf_op jit(solution)/shard_map/ppermute | solution.py:24
  50.3 30.1 %collective-permute-start.15 = (f32[32,24,4]{2,1,0:T(8,128)S(1)}, f32[32,24,4]{2,1,0:T(8,128)S(1)}, u32[]{:S(2)}, u32[]{:S(2)}) collective-permute-start(f32[32,24,4]{2,1,0:T(8,128)S(1)} %get-tuple-element.35), channel_id=1, source_target_pairs={{1,0},{2,1},{3,2},{4,3},{5,4},{6,5},{7,6},{0,7},{9,8},{10,9},{11,1... | collective-permute-start | bytes 36872 | tf_op jit(solution)/shard_map/ppermute | solution.py:27
  87.1 1.7 %copy-start.1 = (f32[32,16,256]{2,1,0:T(8,128)}, f32[32,16,256]{2,1,0:T(8,128)S(1)}, u32[]{:S(2)}) copy-start(f32[32,16,256]{2,1,0:T(8,128)S(1)} %get-tuple-element.28) | copy-start | bytes 1572868
  87.1 1.7 %copy-start.2 = (f32[32,16,256]{2,1,0:T(8,128)}, f32[32,16,256]{2,1,0:T(8,128)S(1)}, u32[]{:S(2)}) copy-start(f32[32,16,256]{2,1,0:T(8,128)S(1)} %get-tuple-element.29) | copy-start | bytes 1572868
where the time goes:
time: 166 us; the launch traced here: 163 us
  blocking collectives  42.4 us (26%)
  waiting for transfers between devices  37.4 us (23%)
  starting transfers between devices  30.1 us (18%)
  between operations  19.6 us (12%)
  other arithmetic  17.3 us (10%)
  local copies, waits for them, and re-layouts  16.4 us (10%)
    psum x5, blocking collectives, by_axis(): return functools.reduce(lax.psum, axes, x)  42.4 us
    ppermute x8, waiting for transfers between devices, extended(): lax.ppermute(lax.slice_in_dim(block, 0, width, axis=dim), axis, backward)  20.5 us
    ppermute x8, starting transfers between devices, extended(): lax.ppermute(lax.slice_in_dim(block, 0, width, axis=dim), axis, backward)  17.5 us
    ppermute x8, waiting for transfers between devices, extended(): lax.ppermute(lax.slice_in_dim(block, block.shape[dim] - width, None, axis...  17 us
    ppermute x8, starting transfers between devices, extended(): lax.ppermute(lax.slice_in_dim(block, block.shape[dim] - width, None, axis...  12.6 us
    concatenate x1, local copies, waits for them, and re-layouts, body(): jnp.concatenate([jnp.stack(squares), jnp.stack(crosses)])  10.7 us
    sub x5, other arithmetic, body(): latest = 2.0 * advance(padded_new) - padded_old[:, 1:-1, 1:-1]  8.54 us
    concatenate x7, other arithmetic, extended(): block = jnp.concatenate([low, block, high], axis=dim)  3.66 us
  transfers between devices with their start and end apart: 16, of which 6 were waited for; matrix products, arithmetic and copies ran while one was open for 3% of the time, Pallas kernels for 0%

commit v1 on v0

v1 whole, which is shorter than its diff:
```python
import functools

import jax
import jax.numpy as jnp
from jax import lax
from jax.experimental import pallas as pl
from jax.experimental.pallas import tpu as pltpu
from jax.sharding import PartitionSpec as P

STEPS = 8
SCALE = 4.6
COUPLING = 2.0 / SCALE
MESH = pl.DeviceIdType.MESH
NQ = 2 * STEPS + 1
NV, RH, CH = 32, 16, 256
PAD = (STEPS + 1) // 2
ROWS = RH + 2 * PAD
SLOTS = NV // 8
SW = 128 // SLOTS
WIDE = STEPS


def roll(x, shift):
    return pltpu.roll(x, shift % 128, axis=x.ndim - 1)


def lanes(shape):
    return lax.broadcasted_iota(jnp.int32, shape, len(shape) - 1)


def kernel(
    sizes, vec_hbm, dis_hbm, prev_out, last_out, mom_out,
    V, F, S, DE, DB, PK, RC, ACC, R1, R2,
    load_sem, out_sem, send_sem, recv_sem, s1_send, s1_recv, s2_send, s2_recv,
):
    GR, ROW, COL = sizes
    COUNT = float(GR * NV * ROW * RH * COL * CH)
    g = lax.axis_index("grp")
    r = lax.axis_index("row")
    c = lax.axis_index("col")
    up, down = lax.rem(r + ROW - 1, ROW), lax.rem(r + 1, ROW)
    left, right = lax.rem(c + COL - 1, COL), lax.rem(c + 1, COL)

    sites = pl.ds(0, NV * RH)
    loads = [
        pltpu.make_async_copy(
            vec_hbm.at[:, pl.ds(128 * h, 128)], V.at[h, sites], load_sem.at[h]
        )
        for h in range(2)
    ]
    loads.append(
        pltpu.make_async_copy(
            dis_hbm, DE.at[pl.ds(8, RH), pl.ds(128, CH)], load_sem.at[2]
        )
    )
    for copy in loads:
        copy.start()

    row_peers = [(g, lax.rem(r + d, ROW), c) for d in range(1, ROW)]
    col_peers = []
    for dg in range(GR):
        for dc in range(COL):
            if dg or dc:
                col_peers.append((lax.rem(g + dg, GR), r, lax.rem(c + dc, COL)))
    corners = [(g, a, b) for a in (up, down) for b in (left, right)]
    barrier = pltpu.get_barrier_semaphore()
    for peer in row_peers + col_peers + corners:
        pl.semaphore_signal(barrier, inc=1, device_id=peer, device_id_type=MESH)

    for copy in loads:
        copy.wait()

    lane8 = lanes((8, 128))
    slot8 = lane8 // SW
    in8 = lane8 % SW

    def own_strips(row):
        m0 = F[0, row, :, 0:128]
        m1 = F[0, row, :, 128:256]
        xl = jnp.zeros((8, 128), jnp.float32)
        xr = jnp.zeros((8, 128), jnp.float32)
        for t in range(SLOTS):
            ml = (slot8 == t) & (in8 >= WIDE) & (in8 < 3 * WIDE)
            mr = (slot8 == t) & (in8 < 2 * WIDE)
            xl = jnp.where(ml, roll(m0[8 * t : 8 * t + 8], SW * t + WIDE), xl)
            xr = jnp.where(mr, roll(m1[8 * t : 8 * t + 8], SW * t + 2 * WIDE), xr)
        return xl, xr

    def strided(i, t):
        return pl.ds(t * 8 * RH + i, 8, stride=RH)

    for i in range(RH):
        for t in range(SLOTS):
            for h in range(2):
                F[0, PAD + i, 8 * t : 8 * t + 8, 128 * h : 128 * h + 128] = V.at[h][
                    strided(i, t), :
                ]

    def pack(a, _):
        pleft = jnp.zeros((8, 128), jnp.float32)
        pright = jnp.zeros((8, 128), jnp.float32)
        for b in range(4):
            row = PAD + 4 * a + b
            xl, xr = own_strips(row)
            S[0, row, :, 0:128] = xl
            S[0, row, :, 128:256] = xr
            m = (in8 // WIDE) == b
            pleft = jnp.where(m, roll(xl, WIDE * b - WIDE), pleft)
            pright = jnp.where(m, roll(xr, WIDE * b - WIDE), pright)
        PK[0, a] = pleft
        PK[1, a] = pright
        return 0

    lax.fori_loop(0, RH // 4, pack, 0)

    pl.semaphore_wait(barrier, len(row_peers) + len(col_peers) + len(corners))

    mid = pl.ds(128, CH)
    plan = [
        (F.at[0, pl.ds(PAD + RH - PAD, PAD)], F.at[0, pl.ds(0, PAD)], (g, down, c)),
        (F.at[0, pl.ds(PAD, PAD)], F.at[0, pl.ds(PAD + RH, PAD)], (g, up, c)),
        (PK.at[1], RC.at[0, pl.ds(1, 4)], (g, r, right)),
        (PK.at[0], RC.at[1, pl.ds(1, 4)], (g, r, left)),
        (PK.at[1, 3], RC.at[0, 0], (g, down, right)),
        (PK.at[1, 0], RC.at[0, 5], (g, up, right)),
        (PK.at[0, 3], RC.at[1, 0], (g, down, left)),
        (PK.at[0, 0], RC.at[1, 5], (g, up, left)),
        (DE.at[pl.ds(16, 8), mid], DE.at[pl.ds(0, 8), mid], (g, down, c)),
        (DE.at[pl.ds(8, 8), mid], DE.at[pl.ds(24, 8), mid], (g, up, c)),
        (DE.at[pl.ds(8, 16), pl.ds(256, 128)], DE.at[pl.ds(8, 16), pl.ds(0, 128)], (g, r, right)),
        (DE.at[pl.ds(8, 16), pl.ds(128, 128)], DE.at[pl.ds(8, 16), pl.ds(384, 128)], (g, r, left)),
        (DE.at[pl.ds(16, 8), pl.ds(256, 128)], DE.at[pl.ds(0, 8), pl.ds(0, 128)], (g, down, right)),
        (DE.at[pl.ds(8, 8), pl.ds(256, 128)], DE.at[pl.ds(24, 8), pl.ds(0, 128)], (g, up, right)),
        (DE.at[pl.ds(16, 8), pl.ds(128, 128)], DE.at[pl.ds(0, 8), pl.ds(384, 128)], (g, down, left)),
        (DE.at[pl.ds(8, 8), pl.ds(128, 128)], DE.at[pl.ds(24, 8), pl.ds(384, 128)], (g, up, left)),
    ]
    halo = [
        pltpu.make_async_remote_copy(
            src_ref=source, dst_ref=target, send_sem=send_sem.at[k], recv_sem=recv_sem.at[k],
            device_id=device, device_id_type=MESH,
        )
        for k, (source, target, device) in enumerate(plan)
    ]
    order = [2, 3, 4, 5, 6, 7, 0, 1] + list(range(8, 16))
    for k in order:
        halo[k].start()

    first_lane = lane8 == 0
    last_lane = lane8 == 127
    even_lane = lane8 % 2 == 0

    def spread_loop(lo, hi):
        for q in range(4):
            rows = [i for i in range(8) if lo <= 8 * q + i - (8 - PAD) < hi]
            if rows:
                x = DE[8 * q : 8 * q + 8, 128:384] * COUPLING
            for i in rows:
                DB[8 * q + i - (8 - PAD), :, 0:256] = jnp.broadcast_to(x[i : i + 1], (8, 256))

    spread_loop(PAD, PAD + RH)

    def update(level, c, vert, old, d, wide):
        if wide:
            c0, c1 = c
            l0 = roll(c0, 1)
            r1 = roll(c1, -1)
            l1 = jnp.where(first_lane, l0, roll(c1, 1))
            r0 = jnp.where(last_lane, r1, roll(c0, -1))
            sides = (l0 + r0, l1 + r1)
        else:
            sides = tuple(roll(x, 1) + roll(x, -1) for x in c)
        out = []
        for k in range(2):
            new = d[k] * c[k] - COUPLING * (sides[k] + vert[k])
            new = 0.5 * new if level == 1 else new - old[k]
            out.append(new)
        return out

    def halves(ref, level, row, t=None):
        if t is None:
            return ref[level, row, :, 0:128], ref[level, row, :, 128:256]
        return ref[level, row, 8 * t : 8 * t + 8, 0:128], ref[level, row, 8 * t : 8 * t + 8, 128:256]

    def one_row(level, row, mask, main, strip, acc):
        if acc is not None:
            acc = list(acc)

        def vertical(ref, t):
            if mask is True:
                return halves(ref, level - 1, row + 1, t)
            if mask is False:
                return halves(ref, level - 1, row - 1, t)
            below = halves(ref, level - 1, row + 1, t)
            above = halves(ref, level - 1, row - 1, t)
            return [jnp.where(mask, below[k], above[k]) for k in range(2)]

        if main:
            d = DB[row, :, 0:128], DB[row, :, 128:256]
            for t in range(SLOTS):
                c = halves(F, level - 1, row, t)
                old = halves(F, level - 2, row, t) if level > 1 else None
                new = update(level, c, vertical(F, t), old, d, True)
                for k in range(2):
                    F[level, row, 8 * t : 8 * t + 8, 128 * k : 128 * k + 128] = new[k]
                    if acc is not None:
                        acc[k] = acc[k] + new[k] * new[k]
                        acc[2 + k] = acc[2 + k] + new[k] * c[k]
        if strip:
            d = DB[row, :, 256:384], DB[row, :, 384:512]
            c = halves(S, level - 1, row)
            old = halves(S, level - 2, row) if level > 1 else None
            new = update(level, c, vertical(S, None), old, d, False)
            for k in range(2):
                S[level, row, :, 128 * k : 128 * k + 128] = new[k]
                if acc is not None:
                    acc[4 + k] = acc[4 + k] + new[k] * new[k]
                    acc[6 + k] = acc[6 + k] + new[k] * c[k]
        return acc

    def parity(row):
        return (lane8 + row) % 2 == 0

    zero = jnp.zeros((8, 128), jnp.float32)
    accs = [[zero] * 8 for _ in range(STEPS + 1)]

    def square0(i, acc):
        acc = list(acc)
        for t in range(SLOTS):
            x = halves(F, 0, i, t)
            for k in range(2):
                acc[k] = acc[k] + x[k] * x[k]
        return tuple(acc)

    a0 = lax.fori_loop(PAD, PAD + RH, square0, (zero, zero), unroll=2)
    accs[0][0:2] = a0

    for n in range(1, STEPS + 1):
        edge = (n + 1) // 2
        lo = PAD + edge
        if n % 2:
            one_row(n, lo - 1, True, True, False, None)
            one_row(n, PAD + RH - edge, False, True, False, None)

        def pair(j, acc, n=n, lo=lo):
            for u in range(2):
                row = lo + 2 * j + u
                mask = even_lane if (lo + u) % 2 == 0 else jnp.logical_not(even_lane)
                acc = one_row(n, row, mask, True, False, tuple(acc) + (zero,) * 4)[:4]
            return tuple(acc)

        a = lax.fori_loop(0, (RH - 2 * edge) // 2, pair, (zero,) * 4)
        accs[n][0:4] = a

    for k in range(16):
        halo[k].wait_recv()

    spread_loop(0, PAD)
    spread_loop(PAD + RH, ROWS)

    for q in range(4):
        for side in range(2):
            rows = pl.ds(8 * q, 8)
            if side == 0:
                a, b = DE[rows, 0:128], DE[rows, 128:256]
                x = jnp.where(lane8 < WIDE, roll(a, WIDE), roll(b, WIDE))
            else:
                a, b = DE[rows, 256:384], DE[rows, 384:512]
                x = jnp.where(lane8 < 2 * WIDE, roll(a, 2 * WIDE), roll(b, 2 * WIDE))
            x = jnp.where(lane8 < 3 * WIDE, x * COUPLING, 0.0)
            x = x + roll(x, SW)
            x = x + roll(x, 2 * SW)
            for i in range(8):
                row = 8 * q + i - (8 - PAD)
                if 0 <= row < ROWS:
                    DB[row, :, 256 + 128 * side : 384 + 128 * side] = jnp.broadcast_to(
                        x[i : i + 1], (8, 128)
                    )

    def strips(a, own):
        gl, gr = RC[0, a], RC[1, a]
        for b in range(4):
            row = 4 * a + b
            if own:
                xl, xr = own_strips(row)
            else:
                xl, xr = halves(S, 0, row)
            xl = jnp.where(in8 < WIDE, roll(gl, -WIDE * b), xl)
            xr = jnp.where(
                (in8 >= 2 * WIDE) & (in8 < 3 * WIDE), roll(gr, 2 * WIDE - WIDE * b), xr
            )
            S[0, row, :, 0:128] = xl
            S[0, row, :, 128:256] = xr

    strips(0, True)
    strips(5, True)

    def strips_mid(a, _):
        strips(a, False)
        return 0

    lax.fori_loop(1, 5, strips_mid, 0)

    for n in range(1, STEPS + 1):
        edge = (n + 1) // 2
        reach = (STEPS + 1 - n) // 2
        top, bottom = PAD - reach, PAD + RH - 1 + reach
        if n % 2:
            one_row(n, top, True, True, True, None)
            one_row(n, bottom, False, True, True, None)
            top += 1

        def outside(i, _, n=n):
            one_row(n, i, parity(i), True, True, None)
            j = ROWS - 1 - i
            one_row(n, j, parity(j), True, True, None)
            return 0

        if top < PAD:
            lax.fori_loop(top, PAD, outside, 0)

        def inside(i, acc, n=n):
            acc = one_row(n, i, parity(i), True, True, acc)
            j = ROWS - 1 - i
            return tuple(one_row(n, j, parity(j), True, True, acc))

        acc = tuple(accs[n])
        acc = lax.fori_loop(PAD, PAD + edge, inside, acc)

        def middle(i, acc, n=n, lo=PAD + edge):
            acc = tuple(acc)
            for u in range(2):
                row = lo + 2 * i + u
                mask = even_lane if (lo + u) % 2 == 0 else jnp.logical_not(even_lane)
                acc = one_row(n, row, mask, False, True, (zero,) * 4 + tuple(acc))[4:]
            return tuple(acc)

        rest = lax.fori_loop(0, (RH - 2 * edge) // 2, middle, acc[4:])
        accs[n] = list(acc[:4]) + list(rest)

    base = []
    for n in range(STEPS + 1):
        own = [
            lane8 >= n,
            lane8 < 128 - n,
            (in8 >= WIDE) & (in8 < WIDE + n),
            (in8 >= 2 * WIDE - n) & (in8 < 2 * WIDE),
        ]
        for kind in range(2):
            if n == 0 and kind == 1:
                continue
            total = zero
            picks = (0, 1, 4, 5) if kind == 0 else (2, 3, 6, 7)
            for m, k in zip(own, picks):
                if n == 0:
                    total = total + accs[n][k]
                else:
                    total = total + jnp.where(m, accs[n][k], 0.0)
            q = 2 * n if kind == 0 else 2 * n - 1
            if q < 2:
                base.append(total)
            else:
                total = 2.0 * total - base[q % 2]
            ACC[q] = total
    for q in range(NQ, 24):
        ACC[q] = zero
    sums = jnp.sum(ACC[...], axis=1)
    totals = jnp.broadcast_to(jnp.sum(sums, axis=1, keepdims=True), (24, 128))
    at = lax.broadcasted_iota(jnp.int32, (24, 128), 0) == lanes((24, 128))
    R1[r] = jnp.sum(jnp.where(at, totals, 0.0), axis=0, keepdims=True)

    def exchange(buf, mine, peers, send, recv):
        return [
            pltpu.make_async_remote_copy(
                src_ref=buf.at[mine], dst_ref=buf.at[mine],
                send_sem=send.at[k], recv_sem=recv.at[k],
                device_id=peer, device_id_type=MESH,
            )
            for k, peer in enumerate(peers)
        ]

    first = exchange(R1, r, row_peers, s1_send, s1_recv)
    for copy in first:
        copy.start()

    for k, level in enumerate((STEPS - 1, STEPS)):
        for i in range(RH):
            xl, xr = halves(S, level, PAD + i)
            for t in range(SLOTS):
                m0, m1 = halves(F, level, PAD + i, t)
                V.at[2 * k][strided(i, t), :] = jnp.where(
                    lane8 < WIDE, roll(xl, -(SW * t + WIDE)), m0
                )
                V.at[2 * k + 1][strided(i, t), :] = jnp.where(
                    lane8 >= 128 - WIDE, roll(xr, 128 - 2 * WIDE - SW * t), m1
                )
    outs = [
        pltpu.make_async_copy(
            V.at[2 * k + h, sites], ref.at[:, pl.ds(128 * h, 128)], out_sem.at[k, h]
        )
        for k, ref in enumerate((prev_out, last_out))
        for h in range(2)
    ]
    for copy in outs:
        copy.start()

    for copy in first:
        copy.wait_recv()
    mine = g * COL + c
    R2[mine] = jnp.sum(R1[...], axis=0)
    second = exchange(R2, mine, col_peers, s2_send, s2_recv)
    for copy in second:
        copy.start()
    for copy in second:
        copy.wait_recv()
    mom_out[...] = jnp.sum(R2[...], axis=0) * (1.0 / COUNT)

    for copy in halo + first + second:
        copy.wait_send()
    for copy in outs:
        copy.wait()


def body(sizes, vectors, disorder):
    GR, ROW, COL = sizes
    f32 = jnp.float32
    dma = pltpu.SemaphoreType.DMA
    hbm = pl.BlockSpec(memory_space=pltpu.HBM)
    prev, last, moments = pl.pallas_call(
        functools.partial(kernel, sizes),
        out_shape=(
            jax.ShapeDtypeStruct((NV * RH, CH), f32),
            jax.ShapeDtypeStruct((NV * RH, CH), f32),
            jax.ShapeDtypeStruct((1, 128), f32),
        ),
        in_specs=[hbm, hbm],
        out_specs=(hbm, hbm, pl.BlockSpec(memory_space=pltpu.VMEM)),
        scratch_shapes=[
            pltpu.VMEM((4, (NV + 1) * RH, 128), f32),
            pltpu.VMEM((STEPS + 1, ROWS, NV, CH), f32),
            pltpu.VMEM((STEPS + 1, ROWS, 8, 256), f32),
            pltpu.VMEM((32, 512), f32),
            pltpu.VMEM((ROWS, 8, 512), f32),
            pltpu.VMEM((2, 4, 8, 128), f32),
            pltpu.VMEM((2, 6, 8, 128), f32),
            pltpu.VMEM((24, 8, 128), f32),
            pltpu.VMEM((ROW, 1, 128), f32),
            pltpu.VMEM((GR * COL, 1, 128), f32),
            dma((3,)),
            dma((2, 2)),
            dma((16,)),
            dma((16,)),
            dma((ROW - 1,)),
            dma((ROW - 1,)),
            dma((GR * COL - 1,)),
            dma((GR * COL - 1,)),
        ],
        compiler_params=pltpu.CompilerParams(
            collective_id=0, has_side_effects=True, vmem_limit_bytes=32 << 20
        ),
    )(vectors.reshape(NV * RH, CH), disorder)
    return prev.reshape(vectors.shape), last.reshape(vectors.shape), moments[0, :NQ]


def solution(mesh):
    sizes = mesh.shape["grp"], mesh.shape["row"], mesh.shape["col"]
    return jax.shard_map(
        functools.partial(body, sizes),
        mesh=mesh,
        in_specs=(P("grp", "row", "col"), P("row", "col")),
        out_specs=(P("grp", "row", "col"), P("grp", "row", "col"), P()),
        check_vma=False,
    )
```

time: 166 us -> 41.5 us (0.25); the launches traced: 163 us -> 41.3 us
  blocking collectives: 42.4 us -> 0 us
  waiting for transfers between devices: 37.4 us -> 0 us
  Pallas kernels: 0 us -> 36.8 us
  starting transfers between devices: 30.1 us -> 0 us
  between operations: 19.6 us -> 0.65 us
  other arithmetic: 17.3 us -> 0 us
  local copies, waits for them, and re-layouts: 16.4 us -> 3.85 us
    psum x5 -> x0, blocking collectives: 42.4 us -> none  [by_axis(): return functools.reduce(lax.psum, axes, x)]
    ppermute x16 -> x0, waiting for transfers between devices: 37.4 us -> none  [the longest x8 20.5 us: extended(): lax.ppermute(lax.slice_in_dim(block, 0, width, axis=dim), axis, backward)]
    pallas_call x0 -> x1, Pallas kernels: none -> 36.8 us  [body(): pl.pallas_call(functools.partial(kernel, sizes), out_shape=(jax.ShapeDtyp...]
    ppermute x16 -> x0, starting transfers between devices: 30.1 us -> none  [the longest x8 17.5 us: extended(): lax.ppermute(lax.slice_in_dim(block, 0, width, axis=dim), axis, backward)]
    concatenate x1 -> x0, local copies, waits for them, and re-layouts: 10.7 us -> none  [body(): jnp.concatenate([jnp.stack(squares), jnp.stack(crosses)])]
    sub x5 -> x0, other arithmetic: 8.54 us -> none  [body(): latest = 2.0 * advance(padded_new) - padded_old[:, 1:-1, 1:-1]]
    slice x16 -> x0, local copies, waits for them, and re-layouts: 3.89 us -> none  [the longest x8 2.63 us: extended(): lax.slice_in_dim(block, block.shape[dim] - width, None, axis=dim)]
    concatenate x7 -> x0, other arithmetic: 3.66 us -> none  [extended(): block = jnp.concatenate([low, block, high], axis=dim)]
  transfers between devices with their start and end apart: 16 -> 0, of which waited for: 6 -> 0; matrix products, arithmetic and copies ran while one was open for 3% -> 0% of each run, Pallas kernels for 0% -> 0%
where the time goes in v1:
time: 41.5 us; the launch traced here: 41.3 us
  Pallas kernels  36.8 us (89%)
  local copies, waits for them, and re-layouts  3.85 us (9%)
  between operations  0.65 us (2%)
    pallas_call x1, Pallas kernels, body(): pl.pallas_call(functools.partial(kernel, sizes), out_shape=(jax.ShapeDtyp...  36.8 us
    unnamed x6, local copies, waits for them, and re-layouts  3.34 us

profile of v1, /device:TPU:1, one launch (start us, length us, event | category | flops | bytes accessed | tf_op | source)
XLA Modules:
  0.0 41.3 jit_solution(13600936187061080099)
XLA Ops:
  0.6 0.0 copy-start
  0.6 1.0 %copy-done = f32[32,16,256]{2,1,0:T(8,128)S(1)} copy-done((f32[32,16,256]{2,1,0:T(8,128)S(1)}, f32[32,16,256]{2,1,0:T(8,128)}, u32[]{:S(2)}) %copy-start) | copy-done | bytes 524312
  1.7 0.0 copy-start.1
  1.7 0.7 %copy-done.1 = f32[16,256]{1,0:T(8,128)S(1)} copy-done((f32[16,256]{1,0:T(8,128)S(1)}, f32[16,256]{1,0:T(8,128)}, u32[]{:S(2)}) %copy-start.1) | copy-done | bytes 16408
  2.4 36.8 %shard_map.49 = (f32[512,256]{1,0:T(8,128)S(1)}, f32[512,256]{1,0:T(8,128)S(1)}, f32[1,128]{1,0:T(1,128)S(1)}) custom-call(f32[512,256]{1,0:T(8,128)S(1)} %bitcast.5, f32[16,256]{1,0:T(8,128)S(1)} %copy-done.1), custom_call_target="tpu_custom_call" | custom-call | tf_op jit(solution)/shard_map/pallas_call | solution.py:428
  39.2 0.5 %slice_bitcast_fusion = f32[17]{0:T(128)} fusion(f32[1,128]{1,0:T(1,128)S(1)} %get-tuple-element.8), kind=kLoop, calls=%fused_computation | loop fusion | bytes 136 | tf_op jit(solution)/shard_map/squeeze | solution.py:461
  39.7 0.8 %copy.7 = f32[32,16,256]{2,1,0:T(8,128)} copy(f32[32,16,256]{2,1,0:T(8,128)S(1)} %bitcast.7) | data formatting | bytes 1048576
  40.5 0.8 %copy.8 = f32[32,16,256]{2,1,0:T(8,128)} copy(f32[32,16,256]{2,1,0:T(8,128)S(1)} %bitcast.6) | data formatting | bytes 1048576
Async XLA Ops:
  0.6 1.0 %copy-start = (f32[32,16,256]{2,1,0:T(8,128)S(1)}, f32[32,16,256]{2,1,0:T(8,128)}, u32[]{:S(2)}) copy-start(f32[32,16,256]{2,1,0:T(8,128)} %param.2) | copy-start | bytes 1572868
  1.7 0.7 %copy-start.1 = (f32[16,256]{1,0:T(8,128)S(1)}, f32[16,256]{1,0:T(8,128)}, u32[]{:S(2)}) copy-start(f32[16,256]{1,0:T(8,128)} %dis_hbm.1) | copy-start | bytes 49156

commit v2 on v1

v2 whole, which is shorter than its diff:
```python
import functools

import jax
import jax.numpy as jnp
from jax import lax
from jax.experimental import pallas as pl
from jax.experimental.pallas import tpu as pltpu
from jax.sharding import PartitionSpec as P

STEPS = 8
SCALE = 4.6
COUPLING = 2.0 / SCALE
MESH = pl.DeviceIdType.MESH
NQ = 2 * STEPS + 1
NV, RH, CH = 32, 16, 256
PAD = (STEPS + 1) // 2
ROWS = RH + 2 * PAD
SLOTS = NV // 8


def roll(x, shift):
    return pltpu.roll(x, shift % 128, axis=1)


def gather(x, index):
    return jnp.take_along_axis(x, index, axis=1, mode="promise_in_bounds")


def half_of(i, kind):
    return (i + kind) % 2


def alone(i, kind, n):
    j = RH - 1 - i
    return n <= (min(2 * i + 1, 2 * j) if kind == 0 else min(2 * i, 2 * j + 1))


def wanted(i, kind, n):
    if i < 0:
        return n <= STEPS + 1 + 2 * i - kind
    if i >= RH:
        return n <= STEPS + 1 - 2 * (i - RH + 1) - (1 - kind)
    return True


def kernel(
    sizes, vec_hbm, dis_hbm, prev_out, last_out, mom_out,
    V, F, S, DE, DB, PK, RC, ACC, SUM, R1, R2,
    load_sem, out_sem, send_sem, recv_sem, s1_send, s1_recv, s2_send, s2_recv,
):
    GR, ROW, COL = sizes
    COUNT = float(GR * NV * ROW * RH * COL * CH)
    g = lax.axis_index("grp")
    r = lax.axis_index("row")
    c = lax.axis_index("col")
    up, down = lax.rem(r + ROW - 1, ROW), lax.rem(r + 1, ROW)
    left, right = lax.rem(c + COL - 1, COL), lax.rem(c + 1, COL)

    sites = pl.ds(0, NV * RH)
    loads = [
        pltpu.make_async_copy(
            vec_hbm.at[:, pl.ds(128 * h, 128)], V.at[h, sites], load_sem.at[h]
        )
        for h in range(2)
    ]
    loads.append(
        pltpu.make_async_copy(
            dis_hbm, DE.at[pl.ds(8, RH), pl.ds(128, CH)], load_sem.at[2]
        )
    )
    for copy in loads:
        copy.start()

    row_peers = [(g, lax.rem(r + d, ROW), c) for d in range(1, ROW)]
    col_peers = []
    for dg in range(GR):
        for dc in range(COL):
            if dg or dc:
                col_peers.append((lax.rem(g + dg, GR), r, lax.rem(c + dc, COL)))
    corners = [(g, a, b) for a in (up, down) for b in (left, right)]
    barrier = pltpu.get_barrier_semaphore()
    for peer in row_peers + col_peers + corners:
        pl.semaphore_signal(barrier, inc=1, device_id=peer, device_id_type=MESH)

    lane = lax.broadcasted_iota(jnp.int32, (8, 128), 1)
    zero = jnp.zeros((8, 128), jnp.float32)
    in16 = lane % 16
    in32 = lane % 32
    is_left = in32 < 16
    low = lane < 64
    pick = ((2 * lane) % 128, (2 * lane + 1) % 128)

    for copy in loads:
        copy.wait()

    def strided(i, t):
        return pl.ds(t * 8 * RH + i, 8, stride=RH)

    def split(m0, m1):
        return [jnp.where(low, gather(m0, p), gather(m1, p)) for p in pick]

    def get(ref, n, row, t, h):
        return ref[n, row, t, :, 128 * h : 128 * h + 128]

    def put(ref, n, row, t, h, x):
        ref[n, row, t, :, 128 * h : 128 * h + 128] = x

    strip_index = jnp.where(
        is_left, jnp.clip(in16 - 4, 0, 127), jnp.clip(120 + in16, 0, 127)
    )
    strip_own = (is_left & (in16 >= 4) & (in16 < 12)) | (~is_left & (in16 < 8))

    def own_strip(parts):
        x = gather(parts[0], strip_index)
        for t in range(1, SLOTS):
            x = jnp.where(lane >= 32 * t, gather(parts[t], strip_index), x)
        return jnp.where(strip_own, x, 0.0)

    order = [0, 1, 2, 3, 12, 13, 14, 15] + list(range(4, 12))
    packed = {}
    for i in order:
        parts = ([], [])
        for t in range(SLOTS):
            halves = split(V.at[0][strided(i, t), :], V.at[1][strided(i, t), :])
            for h in range(2):
                put(F, 0, PAD + i, t, h, halves[h])
                parts[h].append(halves[h])
        for h in range(2):
            x = own_strip(parts[h])
            put(S, 0, PAD + i, 0, h, x)
            a, spot = i // 4, 4 * (2 * (i % 4) + h)
            m = (in32 >= spot) & (in32 < spot + 4)
            for side, edge in ((0, 4), (1, 20)):
                packed[side, a] = jnp.where(m, roll(x, spot - edge), packed.get((side, a), zero))
                if i % 4 == 3 and h == 1:
                    PK[side, a] = packed[side, a]

    pl.semaphore_wait(barrier, len(row_peers) + len(col_peers) + len(corners))

    mid = pl.ds(128, CH)
    plan = [
        (F.at[0, pl.ds(PAD + RH - PAD, PAD)], F.at[0, pl.ds(0, PAD)], (g, down, c)),
        (F.at[0, pl.ds(PAD, PAD)], F.at[0, pl.ds(PAD + RH, PAD)], (g, up, c)),
        (PK.at[1], RC.at[0, pl.ds(1, 4)], (g, r, right)),
        (PK.at[0], RC.at[1, pl.ds(1, 4)], (g, r, left)),
        (PK.at[1, 3], RC.at[0, 0], (g, down, right)),
        (PK.at[1, 0], RC.at[0, 5], (g, up, right)),
        (PK.at[0, 3], RC.at[1, 0], (g, down, left)),
        (PK.at[0, 0], RC.at[1, 5], (g, up, left)),
        (DE.at[pl.ds(16, 8), mid], DE.at[pl.ds(0, 8), mid], (g, down, c)),
        (DE.at[pl.ds(8, 8), mid], DE.at[pl.ds(24, 8), mid], (g, up, c)),
        (DE.at[pl.ds(8, 16), pl.ds(256, 128)], DE.at[pl.ds(8, 16), pl.ds(0, 128)], (g, r, right)),
        (DE.at[pl.ds(8, 16), pl.ds(128, 128)], DE.at[pl.ds(8, 16), pl.ds(384, 128)], (g, r, left)),
        (DE.at[pl.ds(16, 8), pl.ds(256, 128)], DE.at[pl.ds(0, 8), pl.ds(0, 128)], (g, down, right)),
        (DE.at[pl.ds(8, 8), pl.ds(256, 128)], DE.at[pl.ds(24, 8), pl.ds(0, 128)], (g, up, right)),
        (DE.at[pl.ds(16, 8), pl.ds(128, 128)], DE.at[pl.ds(0, 8), pl.ds(384, 128)], (g, down, left)),
        (DE.at[pl.ds(8, 8), pl.ds(128, 128)], DE.at[pl.ds(24, 8), pl.ds(384, 128)], (g, up, left)),
    ]
    halo = [
        pltpu.make_async_remote_copy(
            src_ref=source, dst_ref=target, send_sem=send_sem.at[k], recv_sem=recv_sem.at[k],
            device_id=device, device_id_type=MESH,
        )
        for k, (source, target, device) in enumerate(plan)
    ]
    for k in [0, 1, 4, 5, 6, 7, 2, 3] + list(range(8, 16)):
        halo[k].start()

    def spread_main(lo, hi):
        for q in range(4):
            rows = [i for i in range(8) if lo <= 8 * q + i - 8 < hi]
            if rows:
                x = split(DE[8 * q : 8 * q + 8, 128:256], DE[8 * q : 8 * q + 8, 256:384])
                for h in range(2):
                    y = x[h] * COUPLING
                    for i in rows:
                        DB[8 * q + i - 8 + PAD, :, 128 * h : 128 * h + 128] = jnp.broadcast_to(
                            y[i : i + 1], (8, 128)
                        )

    spread_main(0, RH)

    def advance(ref, n, row, t, kind, d, acc):
        h = half_of(row, kind)
        centre = get(ref, n - 1, row, t, h)
        other = get(ref, n - 1, row, t, 1 - h)
        bond = get(ref, n - 1, row + 1 - 2 * kind, t, h)
        around = other + roll(other, 1 if h == 0 else -1) + bond
        new = d(h) * centre - COUPLING * around
        new = 0.5 * new if n == 1 else new - get(ref, n - 2, row, t, h)
        put(ref, n, row, t, h, new)
        if acc is not None:
            acc[h] = acc[h] + new * new
            acc[2 + h] = acc[2 + h] + new * centre

    def main_d(row):
        return lambda h: DB[row, :, 128 * h : 128 * h + 128]

    for n in range(STEPS + 1):
        for k in range(4):
            ACC[n, k] = zero

    def early(t, _):
        acc = [zero] * 2
        for i in range(RH):
            for h in range(2):
                x = get(F, 0, PAD + i, t, h)
                acc[h] = acc[h] + x * x
        for h in range(2):
            ACC[0, h] = ACC[0, h] + acc[h]
        for n in range(1, STEPS + 1):
            acc = [zero] * 4
            for i in range(RH):
                for kind in range(2):
                    if alone(i, kind, n):
                        advance(F, n, PAD + i, t, kind, main_d(PAD + i), acc)
            for k in range(4):
                ACC[n, k] = ACC[n, k] + acc[k]
        return 0

    lax.fori_loop(0, SLOTS, early, 0)

    for k in range(16):
        halo[k].wait_recv()

    spread_main(-PAD, 0)
    spread_main(RH, RH + PAD)

    left_index = (
        jnp.clip(120 + 2 * in16, 0, 127),
        jnp.clip(121 + 2 * in16, 0, 127),
    )
    left_own = (jnp.clip(2 * in16 - 8, 0, 127), jnp.clip(2 * in16 - 7, 0, 127))
    right_own = (jnp.clip(112 + 2 * in16, 0, 127), jnp.clip(113 + 2 * in16, 0, 127))
    right_index = (jnp.clip(2 * in16 - 16, 0, 127), jnp.clip(2 * in16 - 15, 0, 127))
    for q in range(4):
        parts = [DE[8 * q : 8 * q + 8, 128 * k : 128 * k + 128] for k in range(4)]
        for h in range(2):
            x = jnp.where(
                is_left,
                jnp.where(in16 < 4, gather(parts[0], left_index[h]), gather(parts[1], left_own[h])),
                jnp.where(in16 < 8, gather(parts[2], right_own[h]), gather(parts[3], right_index[h])),
            )
            x = jnp.where(in16 < 12, x * COUPLING, 0.0)
            for i in range(8):
                row = 8 * q + i - 8 + PAD
                if 0 <= row < ROWS:
                    DB[row, :, 256 + 128 * h : 384 + 128 * h] = jnp.broadcast_to(
                        x[i : i + 1], (8, 128)
                    )

    for a in range(6):
        from_left, from_right = RC[0, a], RC[1, a]
        for b in range(4):
            row = 4 * a + b
            for h in range(2):
                if 1 <= a <= 4:
                    x = get(S, 0, row, 0, h)
                else:
                    x = own_strip([get(F, 0, row, t, h) for t in range(SLOTS)])
                spot = 4 * (2 * b + h)
                x = jnp.where(in32 < 4, roll(from_left, -spot), x)
                x = jnp.where((in32 >= 24) & (in32 < 28), roll(from_right, 24 - spot), x)
                put(S, 0, row, 0, h, x)

    def late(u, _):
        for n in range(1, STEPS + 1):
            acc = [zero] * 4
            for row in range(ROWS):
                i = row - PAD
                for kind in range(2):
                    if wanted(i, kind, n) and not (0 <= i < RH and alone(i, kind, n)):
                        for v in range(2):
                            advance(
                                F, n, row, 2 * u + v, kind, main_d(row),
                                acc if 0 <= i < RH else None,
                            )
            for k in range(4):
                ACC[n, k] = ACC[n, k] + acc[k]
        return 0

    lax.fori_loop(0, SLOTS // 2, late, 0)

    strip_acc = {}
    for n in range(1, STEPS + 1):
        acc = [zero] * 4
        for row in range(ROWS):
            i = row - PAD
            for kind in range(2):
                if wanted(i, kind, n):
                    advance(
                        S, n, row, 0, kind,
                        lambda h, row=row: DB[row, :, 256 + 128 * h : 384 + 128 * h],
                        acc if 0 <= i < RH else None,
                    )
        strip_acc[n] = acc

    base = []
    for n in range(STEPS + 1):
        for kind in range(2):
            if n == 0 and kind == 1:
                continue
            total = zero
            for h in range(2):
                x = ACC[n, 2 * kind + h]
                if n:
                    col = 2 * lane + h
                    x = jnp.where((col >= n) & (col < CH - n), x, 0.0)
                    col = jnp.where(is_left, 2 * (in16 - 4) + h, CH - 16 + 2 * in16 + h)
                    near = (col >= 0) & (col < CH) & ((is_left & (col < n)) | (~is_left & (col >= CH - n)))
                    x = x + jnp.where(near, strip_acc[n][2 * kind + h], 0.0)
                total = total + x
            q = 2 * n if kind == 0 else 2 * n - 1
            if q < 2:
                base.append(total)
            else:
                total = 2.0 * total - base[q % 2]
            SUM[q] = total
    for q in range(NQ, 24):
        SUM[q] = zero
    sums = jnp.sum(SUM[...], axis=1)
    totals = jnp.broadcast_to(jnp.sum(sums, axis=1, keepdims=True), (24, 128))
    at = lax.broadcasted_iota(jnp.int32, (24, 128), 0) == lax.broadcasted_iota(
        jnp.int32, (24, 128), 1
    )
    R1[r] = jnp.sum(jnp.where(at, totals, 0.0), axis=0, keepdims=True)

    def exchange(buf, mine, peers, send, recv):
        return [
            pltpu.make_async_remote_copy(
                src_ref=buf.at[mine], dst_ref=buf.at[mine],
                send_sem=send.at[k], recv_sem=recv.at[k],
                device_id=peer, device_id_type=MESH,
            )
            for k, peer in enumerate(peers)
        ]

    outs = [
        pltpu.make_async_copy(
            V.at[2 * k + h, sites], ref.at[:, pl.ds(128 * h, 128)], out_sem.at[k, h]
        )
        for k, ref in enumerate((prev_out, last_out))
        for h in range(2)
    ]
    weave = (lane // 2, 64 + lane // 2)
    is_even = lane % 2 == 0
    outer = (lane < 4) | (lane >= 124)

    def result(k, level):
        def one(i, _):
            strip = [get(S, level, PAD + i, 0, h) for h in range(2)]
            for t in range(SLOTS):
                index = jnp.clip(
                    jnp.where(lane < 4, 32 * t + 4 + lane, 32 * t + 20 - 124 + lane), 0, 127
                )
                x = [
                    jnp.where(outer, gather(strip[h], index), get(F, level, PAD + i, t, h))
                    for h in range(2)
                ]
                for w in range(2):
                    V.at[2 * k + w][strided(i, t), :] = jnp.where(
                        is_even, gather(x[0], weave[w]), gather(x[1], weave[w])
                    )
            return 0

        for i in range(RH):
            one(i, 0)
        for copy in outs[2 * k : 2 * k + 2]:
            copy.start()

    first = exchange(R1, r, row_peers, s1_send, s1_recv)
    for copy in first:
        copy.start()
    result(0, STEPS - 1)
    for copy in first:
        copy.wait_recv()
    mine = g * COL + c
    R2[mine] = jnp.sum(R1[...], axis=0)
    second = exchange(R2, mine, col_peers, s2_send, s2_recv)
    for copy in second:
        copy.start()
    result(1, STEPS)
    for copy in second:
        copy.wait_recv()
    mom_out[...] = jnp.sum(R2[...], axis=0) * (1.0 / COUNT)

    for copy in halo + first + second:
        copy.wait_send()
    for copy in outs:
        copy.wait()


def body(sizes, vectors, disorder):
    GR, ROW, COL = sizes
    f32 = jnp.float32
    dma = pltpu.SemaphoreType.DMA
    hbm = pl.BlockSpec(memory_space=pltpu.HBM)
    prev, last, moments = pl.pallas_call(
        functools.partial(kernel, sizes),
        out_shape=(
            jax.ShapeDtypeStruct((NV * RH, CH), f32),
            jax.ShapeDtypeStruct((NV * RH, CH), f32),
            jax.ShapeDtypeStruct((1, 128), f32),
        ),
        in_specs=[hbm, hbm],
        out_specs=(
            pl.BlockSpec(memory_space=pl.ANY),
            pl.BlockSpec(memory_space=pl.ANY),
            pl.BlockSpec(memory_space=pltpu.VMEM),
        ),
        scratch_shapes=[
            pltpu.VMEM((4, (NV + 1) * RH, 128), f32),
            pltpu.VMEM((STEPS + 1, ROWS, SLOTS, 8, CH), f32),
            pltpu.VMEM((STEPS + 1, ROWS, 1, 8, 256), f32),
            pltpu.VMEM((32, 512), f32),
            pltpu.VMEM((ROWS, 8, 512), f32),
            pltpu.VMEM((2, 4, 8, 128), f32),
            pltpu.VMEM((2, 6, 8, 128), f32),
            pltpu.VMEM((STEPS + 1, 4, 8, 128), f32),
            pltpu.VMEM((24, 8, 128), f32),
            pltpu.VMEM((ROW, 1, 128), f32),
            pltpu.VMEM((GR * COL, 1, 128), f32),
            dma((3,)),
            dma((2, 2)),
            dma((16,)),
            dma((16,)),
            dma((ROW - 1,)),
            dma((ROW - 1,)),
            dma((GR * COL - 1,)),
            dma((GR * COL - 1,)),
        ],
        compiler_params=pltpu.CompilerParams(
            collective_id=0, has_side_effects=True, vmem_limit_bytes=32 << 20
        ),
    )(
        pltpu.with_memory_space_constraint(vectors.reshape(NV * RH, CH), pltpu.HBM),
        pltpu.with_memory_space_constraint(disorder, pltpu.HBM),
    )
    return prev.reshape(vectors.shape), last.reshape(vectors.shape), moments[0, :NQ]


def solution(mesh):
    sizes = mesh.shape["grp"], mesh.shape["row"], mesh.shape["col"]
    return jax.shard_map(
        functools.partial(body, sizes),
        mesh=mesh,
        in_specs=(P("grp", "row", "col"), P("row", "col")),
        out_specs=(P("grp", "row", "col"), P("grp", "row", "col"), P()),
        check_vma=False,
    )
```

time: 41.5 us -> 31.1 us (0.75)
  Pallas kernels: 36.8 us -> 28.3 us
  local copies, waits for them, and re-layouts: 3.85 us -> 2.1 us
    pallas_call x1, Pallas kernels: 36.8 us -> 28.3 us  [body(): pl.pallas_call(functools.partial(kernel, sizes), out_shape=(jax.ShapeDtyp...]
    unnamed x6 -> x2, local copies, waits for them, and re-layouts: 3.34 us -> 1.59 us
where the time goes in v2:
time: 31.1 us; the launch traced here: 31 us
  Pallas kernels  28.3 us (91%)
  local copies, waits for them, and re-layouts  2.1 us (7%)
  between operations  0.64 us (2%)
    pallas_call x1, Pallas kernels, body(): pl.pallas_call(functools.partial(kernel, sizes), out_shape=(jax.ShapeDtyp...  28.3 us
    unnamed x2, local copies, waits for them, and re-layouts  1.59 us

profile of v2, /device:TPU:1, one launch (start us, length us, event | category | flops | bytes accessed | tf_op | source)
XLA Modules:
  0.0 31.0 jit_solution(8256067601076105521)
XLA Ops:
  0.6 28.3 %shard_map.49 = (f32[512,256]{1,0:T(8,128)S(1)}, f32[512,256]{1,0:T(8,128)S(1)}, f32[1,128]{1,0:T(1,128)S(1)}) custom-call(f32[512,256]{1,0:T(8,128)} %bitcast.7, f32[16,256]{1,0:T(8,128)} %dis_hbm.1), custom_call_target="tpu_custom_call" | custom-call | tf_op jit(solution)/shard_map/pallas_call | solution.py:398
  28.9 0.5 %slice_bitcast_fusion = f32[17]{0:T(128)} fusion(f32[1,128]{1,0:T(1,128)S(1)} %get-tuple-element.8), kind=kLoop, calls=%fused_computation | loop fusion | bytes 136 | tf_op jit(solution)/shard_map/squeeze | solution.py:439
  29.4 0.8 %copy.7 = f32[32,16,256]{2,1,0:T(8,128)} copy(f32[32,16,256]{2,1,0:T(8,128)S(1)} %bitcast.6) | data formatting | bytes 1048576
  30.2 0.8 %copy.8 = f32[32,16,256]{2,1,0:T(8,128)} copy(f32[32,16,256]{2,1,0:T(8,128)S(1)} %bitcast.5) | data formatting | bytes 1048576

commit v3 on v2

--- a/solution.py
+++ b/solution.py
@@ -26,6 +26,16 @@
     return jnp.take_along_axis(x, index, axis=1, mode="promise_in_bounds")
 
 
+def permuted(x, matrix):
+    n = x.shape[0]
+    parts = []
+    for _ in range(3):
+        parts.append(x.astype(jnp.bfloat16))
+        x = x - parts[-1].astype(jnp.float32)
+    y = jnp.dot(jnp.concatenate(parts, axis=0), matrix, preferred_element_type=jnp.float32)
+    return y[:n] + y[n : 2 * n] + y[2 * n :]
+
+
 def half_of(i, kind):
     return (i + kind) % 2
 
@@ -45,7 +55,7 @@
 
 def kernel(
     sizes, vec_hbm, dis_hbm, prev_out, last_out, mom_out,
-    V, F, S, DE, DB, PK, RC, ACC, SUM, R1, R2,
+    V, F, S, DE, DB, PK, RC, ACC, SUM, R1, R2, PERM,
     load_sem, out_sem, send_sem, recv_sem, s1_send, s1_recv, s2_send, s2_recv,
 ):
     GR, ROW, COL = sizes
@@ -71,7 +81,7 @@
     for copy in loads:
         copy.start()
 
-    row_peers = [(g, lax.rem(r + d, ROW), c) for d in range(1, ROW)]
+    row_peers = [(g, lax.rem(r + d, ROW), c) for d in sorted(range(1, ROW), key=lambda d: (-min(d, ROW - d), d))]
     col_peers = []
     for dg in range(GR):
         for dc in range(COL):
@@ -90,6 +100,14 @@
     low = lane < 64
     pick = ((2 * lane) % 128, (2 * lane + 1) % 128)
 
+    source = lax.broadcasted_iota(jnp.int32, (CH, CH), 0)
+    target = lax.broadcasted_iota(jnp.int32, (CH, CH), 1)
+    half = CH // 2
+    to_halves = jnp.where(target < half, 2 * target, 2 * target - CH + 1) == source
+    to_columns = jnp.where(source < half, 2 * source, 2 * source - CH + 1) == target
+    for k, pick_one in enumerate((to_halves, to_columns)):
+        PERM[k] = jnp.where(pick_one, 1.0, 0.0).astype(jnp.bfloat16)
+
     for copy in loads:
         copy.wait()
 
@@ -116,15 +134,26 @@
             x = jnp.where(lane >= 32 * t, gather(parts[t], strip_index), x)
         return jnp.where(strip_own, x, 0.0)
 
+    chunk = 64
+
+    def to_parity(k, _):
+        at = pl.ds(pl.multiple_of(chunk * k, chunk), chunk)
+        y = permuted(jnp.concatenate([V[0, at, :], V[1, at, :]], axis=1), PERM[0])
+        V[2, at, :] = y[:, :128]
+        V[3, at, :] = y[:, 128:]
+        return 0
+
+    lax.fori_loop(0, NV * RH // chunk, to_parity, 0)
+
     order = [0, 1, 2, 3, 12, 13, 14, 15] + list(range(4, 12))
     packed = {}
     for i in order:
         parts = ([], [])
         for t in range(SLOTS):
-            halves = split(V.at[0][strided(i, t), :], V.at[1][strided(i, t), :])
             for h in range(2):
-                put(F, 0, PAD + i, t, h, halves[h])
-                parts[h].append(halves[h])
+                x = V.at[2 + h][strided(i, t), :]
+                put(F, 0, PAD + i, t, h, x)
+                parts[h].append(x)
         for h in range(2):
             x = own_strip(parts[h])
             put(S, 0, PAD + i, 0, h, x)
@@ -163,7 +192,7 @@
         )
         for k, (source, target, device) in enumerate(plan)
     ]
-    for k in [0, 1, 4, 5, 6, 7, 2, 3] + list(range(8, 16)):
+    for k in [4, 5, 6, 7, 2, 3, 12, 13, 14, 15, 10, 11, 0, 1, 8, 9]:
         halo[k].start()
 
     def spread_main(lo, hi):
@@ -220,11 +249,34 @@
 
     lax.fori_loop(0, SLOTS, early, 0)
 
-    for k in range(16):
+    by_row = [0, 1, 8, 9]
+    for k in by_row:
         halo[k].wait_recv()
 
     spread_main(-PAD, 0)
     spread_main(RH, RH + PAD)
+
+    def late(u, _):
+        for n in range(1, STEPS + 1):
+            acc = [zero] * 4
+            for row in range(ROWS):
+                i = row - PAD
+                for kind in range(2):
+                    if wanted(i, kind, n) and not (0 <= i < RH and alone(i, kind, n)):
+                        for v in range(2):
+                            advance(
+                                F, n, row, 2 * u + v, kind, main_d(row),
+                                acc if 0 <= i < RH else None,
+                            )
+            for k in range(4):
+                ACC[n, k] = ACC[n, k] + acc[k]
+        return 0
+
+    lax.fori_loop(0, SLOTS // 2, late, 0)
+
+    for k in range(16):
+        if k not in by_row:
+            halo[k].wait_recv()
 
     left_index = (
         jnp.clip(120 + 2 * in16, 0, 127),
@@ -262,24 +314,6 @@
                 x = jnp.where(in32 < 4, roll(from_left, -spot), x)
                 x = jnp.where((in32 >= 24) & (in32 < 28), roll(from_right, 24 - spot), x)
                 put(S, 0, row, 0, h, x)
-
-    def late(u, _):
-        for n in range(1, STEPS + 1):
-            acc = [zero] * 4
-            for row in range(ROWS):
-                i = row - PAD
-                for kind in range(2):
-                    if wanted(i, kind, n) and not (0 <= i < RH and alone(i, kind, n)):
-                        for v in range(2):
-                            advance(
-                                F, n, row, 2 * u + v, kind, main_d(row),
-                                acc if 0 <= i < RH else None,
-                            )
-            for k in range(4):
-                ACC[n, k] = ACC[n, k] + acc[k]
-        return 0
-
-    lax.fori_loop(0, SLOTS // 2, late, 0)
 
     strip_acc = {}
     for n in range(1, STEPS + 1):
@@ -342,29 +376,34 @@
         for k, ref in enumerate((prev_out, last_out))
         for h in range(2)
     ]
-    weave = (lane // 2, 64 + lane // 2)
-    is_even = lane % 2 == 0
     outer = (lane < 4) | (lane >= 124)
 
     def result(k, level):
-        def one(i, _):
-            strip = [get(S, level, PAD + i, 0, h) for h in range(2)]
-            for t in range(SLOTS):
-                index = jnp.clip(
-                    jnp.where(lane < 4, 32 * t + 4 + lane, 32 * t + 20 - 124 + lane), 0, 127
-                )
-                x = [
-                    jnp.where(outer, gather(strip[h], index), get(F, level, PAD + i, t, h))
-                    for h in range(2)
-                ]
-                for w in range(2):
-                    V.at[2 * k + w][strided(i, t), :] = jnp.where(
-                        is_even, gather(x[0], weave[w]), gather(x[1], weave[w])
+        def four(a, _):
+            rows = []
+            for b in range(4):
+                row = PAD + 4 * a + b
+                strip = [get(S, level, row, 0, h) for h in range(2)]
+                for t in range(SLOTS):
+                    index = jnp.clip(
+                        jnp.where(lane < 4, 32 * t + 4 + lane, 32 * t + 20 - 124 + lane), 0, 127
                     )
+                    x = [
+                        jnp.where(outer, gather(strip[h], index), get(F, level, row, t, h))
+                        for h in range(2)
+                    ]
+                    rows.append(jnp.concatenate(x, axis=1))
+            y = permuted(jnp.concatenate(rows, axis=0), PERM[1])
+            for b in range(4):
+                for t in range(SLOTS):
+                    at = NV * b + 8 * t
+                    for w in range(2):
+                        V.at[2 * k + w][strided(4 * a + b, t), :] = y[
+                            at : at + 8, 128 * w : 128 * w + 128
+                        ]
             return 0
 
-        for i in range(RH):
-            one(i, 0)
+        lax.fori_loop(0, RH // 4, four, 0)
         for copy in outs[2 * k : 2 * k + 2]:
             copy.start()
 
@@ -372,6 +411,8 @@
     for copy in first:
         copy.start()
     result(0, STEPS - 1)
+    for copy in halo:
+        copy.wait_send()
     for copy in first:
         copy.wait_recv()
     mine = g * COL + c
@@ -380,13 +421,29 @@
     for copy in second:
         copy.start()
     result(1, STEPS)
+    for copy in first:
+        copy.wait_send()
     for copy in second:
         copy.wait_recv()
     mom_out[...] = jnp.sum(R2[...], axis=0) * (1.0 / COUNT)
 
-    for copy in halo + first + second:
+    for copy in second:
         copy.wait_send()
     for copy in outs:
+        copy.wait()
+
+
+def store(prev, last, sums, prev_out, last_out, mom_out, row, sem):
+    copies = [
+        pltpu.make_async_copy(prev, prev_out, sem.at[0]),
+        pltpu.make_async_copy(last, last_out, sem.at[1]),
+    ]
+    for copy in copies:
+        copy.start()
+    row[...] = sums[0, :NQ]
+    copies.append(pltpu.make_async_copy(row, mom_out, sem.at[2]))
+    copies[2].start()
+    for copy in copies:
         copy.wait()
 
 
@@ -420,6 +477,7 @@
             pltpu.VMEM((24, 8, 128), f32),
             pltpu.VMEM((ROW, 1, 128), f32),
             pltpu.VMEM((GR * COL, 1, 128), f32),
+            pltpu.VMEM((2, CH, CH), jnp.bfloat16),
             dma((3,)),
             dma((2, 2)),
             dma((16,)),
@@ -436,7 +494,20 @@
         pltpu.with_memory_space_constraint(vectors.reshape(NV * RH, CH), pltpu.HBM),
         pltpu.with_memory_space_constraint(disorder, pltpu.HBM),
     )
-    return prev.reshape(vectors.shape), last.reshape(vectors.shape), moments[0, :NQ]
+    anywhere = pl.BlockSpec(memory_space=pl.ANY)
+    prev, last, moments = pl.pallas_call(
+        store,
+        out_shape=(
+            jax.ShapeDtypeStruct((NV * RH, CH), f32),
+            jax.ShapeDtypeStruct((NV * RH, CH), f32),
+            jax.ShapeDtypeStruct((NQ,), f32),
+        ),
+        in_specs=[anywhere, anywhere, pl.BlockSpec(memory_space=pltpu.VMEM)],
+        out_specs=(anywhere, anywhere, anywhere),
+        scratch_shapes=[pltpu.VMEM((NQ,), f32), dma((3,))],
+        compiler_params=pltpu.CompilerParams(vmem_limit_bytes=1 << 20),
+    )(prev, last, moments)
+    return prev.reshape(vectors.shape), last.reshape(vectors.shape), moments
 
 
 def solution(mesh):

time: 31.1 us -> 28.5 us (0.916)
  local copies, waits for them, and re-layouts: 2.1 us -> 0 us
  Pallas kernels: 28.3 us -> 27.7 us
    unnamed x2 -> x0, local copies, waits for them, and re-layouts: 1.59 us -> none
    pallas_call x1, Pallas kernels: 28.3 us -> 26.7 us  [body(): pl.pallas_call(functools.partial(kernel, sizes), out_shape=(jax.ShapeDtyp...]
    pallas_call x0 -> x1, Pallas kernels: none -> 1 us  [body(): pl.pallas_call(store, out_shape=(jax.ShapeDtypeStruct((NV * RH, CH), f32)...]
    squeeze x1 -> x0, local copies, waits for them, and re-layouts: 0.51 us -> none  [body(): moments[0, :NQ]]
where the time goes in v3:
time: 28.5 us; the launch traced here: 28.4 us
  Pallas kernels  27.7 us (97%)
  between operations  0.64 us (2%)
    pallas_call x1, Pallas kernels, body(): pl.pallas_call(functools.partial(kernel, sizes), out_shape=(jax.ShapeDtyp...  26.7 us
    pallas_call x1, Pallas kernels, body(): pl.pallas_call(store, out_shape=(jax.ShapeDtypeStruct((NV * RH, CH), f32)...  1 us

profile of v3, /device:TPU:1, one launch (start us, length us, event | category | flops | bytes accessed | tf_op | source)
XLA Modules:
  0.0 28.4 jit_solution(12268288870781775155)
XLA Ops:
  0.6 26.7 %shard_map.49 = (f32[512,256]{1,0:T(8,128)S(1)}, f32[512,256]{1,0:T(8,128)S(1)}, f32[1,128]{1,0:T(1,128)S(1)}) custom-call(f32[512,256]{1,0:T(8,128)} %bitcast.3, f32[16,256]{1,0:T(8,128)} %dis_hbm.1), custom_call_target="tpu_custom_call" | custom-call | tf_op jit(solution)/shard_map/pallas_call | solution.py:455
  27.4 1.0 %shard_map.50 = (f32[512,256]{1,0:T(8,128)}, f32[512,256]{1,0:T(8,128)}, f32[17]{0:T(128)}) custom-call(f32[512,256]{1,0:T(8,128)S(1)} %get-tuple-element.9.prev, f32[512,256]{1,0:T(8,128)S(1)} %get-tuple-element.10.last, f32[1,128]{1,0:T(1,128)S(1)} %get-tuple-element.11.sums), custom_call_target="tpu_custom_call" | custom-call | tf_op jit(solution)/shard_map/pallas_call | solution.py:498

commit v4 on v3

--- a/solution.py
+++ b/solution.py
@@ -83,8 +83,8 @@
 
     row_peers = [(g, lax.rem(r + d, ROW), c) for d in sorted(range(1, ROW), key=lambda d: (-min(d, ROW - d), d))]
     col_peers = []
-    for dg in range(GR):
-        for dc in range(COL):
+    for dg in reversed(range(GR)):
+        for dc in sorted(range(COL), key=lambda d: (-min(d, COL - d), d)):
             if dg or dc:
                 col_peers.append((lax.rem(g + dg, GR), r, lax.rem(c + dc, COL)))
     corners = [(g, a, b) for a in (up, down) for b in (left, right)]
@@ -134,7 +134,7 @@
             x = jnp.where(lane >= 32 * t, gather(parts[t], strip_index), x)
         return jnp.where(strip_own, x, 0.0)
 
-    chunk = 64
+    chunk = 128
 
     def to_parity(k, _):
         at = pl.ds(pl.multiple_of(chunk * k, chunk), chunk)
@@ -146,23 +146,10 @@
     lax.fori_loop(0, NV * RH // chunk, to_parity, 0)
 
     order = [0, 1, 2, 3, 12, 13, 14, 15] + list(range(4, 12))
-    packed = {}
     for i in order:
-        parts = ([], [])
         for t in range(SLOTS):
             for h in range(2):
-                x = V.at[2 + h][strided(i, t), :]
-                put(F, 0, PAD + i, t, h, x)
-                parts[h].append(x)
-        for h in range(2):
-            x = own_strip(parts[h])
-            put(S, 0, PAD + i, 0, h, x)
-            a, spot = i // 4, 4 * (2 * (i % 4) + h)
-            m = (in32 >= spot) & (in32 < spot + 4)
-            for side, edge in ((0, 4), (1, 20)):
-                packed[side, a] = jnp.where(m, roll(x, spot - edge), packed.get((side, a), zero))
-                if i % 4 == 3 and h == 1:
-                    PK[side, a] = packed[side, a]
+                put(F, 0, PAD + i, t, h, V.at[2 + h][strided(i, t), :])
 
     pl.semaphore_wait(barrier, len(row_peers) + len(col_peers) + len(corners))
 
@@ -192,7 +179,22 @@
         )
         for k, (source, target, device) in enumerate(plan)
     ]
-    for k in [4, 5, 6, 7, 2, 3, 12, 13, 14, 15, 10, 11, 0, 1, 8, 9]:
+    for k in [0, 1, 8, 9]:
+        halo[k].start()
+
+    packed = {}
+    for i in order:
+        for h in range(2):
+            x = own_strip([get(F, 0, PAD + i, t, h) for t in range(SLOTS)])
+            put(S, 0, PAD + i, 0, h, x)
+            a, spot = i // 4, 4 * (2 * (i % 4) + h)
+            m = (in32 >= spot) & (in32 < spot + 4)
+            for side, edge in ((0, 4), (1, 20)):
+                packed[side, a] = jnp.where(m, roll(x, spot - edge), packed.get((side, a), zero))
+                if i % 4 == 3 and h == 1:
+                    PK[side, a] = packed[side, a]
+
+    for k in [4, 5, 6, 7, 2, 3, 12, 13, 14, 15, 10, 11]:
         halo[k].start()
 
     def spread_main(lo, hi):
@@ -229,12 +231,13 @@
         for k in range(4):
             ACC[n, k] = zero
 
-    def early(t, _):
+    def early(u, _):
         acc = [zero] * 2
         for i in range(RH):
-            for h in range(2):
-                x = get(F, 0, PAD + i, t, h)
-                acc[h] = acc[h] + x * x
+            for v in range(2):
+                for h in range(2):
+                    x = get(F, 0, PAD + i, 2 * u + v, h)
+                    acc[h] = acc[h] + x * x
         for h in range(2):
             ACC[0, h] = ACC[0, h] + acc[h]
         for n in range(1, STEPS + 1):
@@ -242,12 +245,13 @@
             for i in range(RH):
                 for kind in range(2):
                     if alone(i, kind, n):
-                        advance(F, n, PAD + i, t, kind, main_d(PAD + i), acc)
+                        for v in range(2):
+                            advance(F, n, PAD + i, 2 * u + v, kind, main_d(PAD + i), acc)
             for k in range(4):
                 ACC[n, k] = ACC[n, k] + acc[k]
         return 0
 
-    lax.fori_loop(0, SLOTS, early, 0)
+    lax.fori_loop(0, SLOTS // 2, early, 0)
 
     by_row = [0, 1, 8, 9]
     for k in by_row:
@@ -273,6 +277,10 @@
         return 0
 
     lax.fori_loop(0, SLOTS // 2, late, 0)
+
+    for row in [*range(PAD), *range(PAD + RH, ROWS)]:
+        for h in range(2):
+            put(S, 0, row, 0, h, own_strip([get(F, 0, row, t, h) for t in range(SLOTS)]))
 
     for k in range(16):
         if k not in by_row:
@@ -306,10 +314,7 @@
         for b in range(4):
             row = 4 * a + b
             for h in range(2):
-                if 1 <= a <= 4:
-                    x = get(S, 0, row, 0, h)
-                else:
-                    x = own_strip([get(F, 0, row, t, h) for t in range(SLOTS)])
+                x = get(S, 0, row, 0, h)
                 spot = 4 * (2 * b + h)
                 x = jnp.where(in32 < 4, roll(from_left, -spot), x)
                 x = jnp.where((in32 >= 24) & (in32 < 28), roll(from_right, 24 - spot), x)

time: 28.5 us -> 28.5 us (level)
  no operation moved by 1% of the time
where the time goes in v4:
time: 28.5 us; the launch traced here: 28.4 us
  Pallas kernels  27.8 us (98%)
  between operations  0.64 us (2%)
    pallas_call x1, Pallas kernels, body(): pl.pallas_call(functools.partial(kernel, sizes), out_shape=(jax.ShapeDtyp...  26.8 us
    pallas_call x1, Pallas kernels, body(): pl.pallas_call(store, out_shape=(jax.ShapeDtypeStruct((NV * RH, CH), f32)...  1 us

profile of v4, /device:TPU:1, one launch (start us, length us, event | category | flops | bytes accessed | tf_op | source)
XLA Modules:
  0.0 28.4 jit_solution(6691772603571552207)
XLA Ops:
  0.6 26.8 %shard_map.49 = (f32[512,256]{1,0:T(8,128)S(1)}, f32[512,256]{1,0:T(8,128)S(1)}, f32[1,128]{1,0:T(1,128)S(1)}) custom-call(f32[512,256]{1,0:T(8,128)} %bitcast.3, f32[16,256]{1,0:T(8,128)} %dis_hbm.1), custom_call_target="tpu_custom_call" | custom-call | tf_op jit(solution)/shard_map/pallas_call | solution.py:460
  27.4 1.0 %shard_map.50 = (f32[512,256]{1,0:T(8,128)}, f32[512,256]{1,0:T(8,128)}, f32[17]{0:T(128)}) custom-call(f32[512,256]{1,0:T(8,128)S(1)} %get-tuple-element.9.prev, f32[512,256]{1,0:T(8,128)S(1)} %get-tuple-element.10.last, f32[1,128]{1,0:T(1,128)S(1)} %get-tuple-element.11.sums), custom_call_target="tpu_custom_call" | custom-call | tf_op jit(solution)/shard_map/pallas_call | solution.py:503
